TPU v7x, 256 devices: a whole 4x4x8 slice. The times are simulated.
256 devices in a mesh: dp: 4 (over x), expert: 64 (over z, y, core).
Axes of the slice: x: 4, y: 4, z: 8, core: 2. Of those that a mesh axis runs over, the one named last changes fastest.
Arguments:
- queries: bfloat16 [16384, 2048], P('expert', 'dp'), may hold values from -160 to 160
- kv_pool: bfloat16 [2, 1024, 64, 2048], P(None, 'expert', None, 'dp'), may hold values from -6 to 6
- page_table: int32 [256, 4], P('expert'), may hold values from 0 to 1023, as said below
- ctx_lens: int32 [16384], P('expert'), may hold values from 2 to 256, as said below
- w_out: bfloat16 [2048, 2048], P('dp', 'expert'), may hold values from -0.59765625 to 0.59765625
- residual: bfloat16 [16384, 2048], P(('expert', 'dp')), may hold values from -3 to 3
- moe_gain: float32 [2048], replicated, may hold values from 0.25 to 1.75
- expert_ids: int32 [16384, 6], P(('expert', 'dp')), may hold values from 0 to 63, all different within a row; in each aligned block of 64 rows (0 to 63, 64 to 127, ...) at most 12 rows name the same one
- route_weights: float32 [16384, 6], P(('expert', 'dp')), may hold values from 0.05 to 0.4
- w_gate: bfloat16 [64, 2048, 1408], P('expert', 'dp'), may hold values from -0.125 to 0.125
- w_up: bfloat16 [64, 2048, 1408], P('expert', 'dp'), may hold values from -0.125 to 0.125
- w_down: bfloat16 [64, 1408, 2048], P('expert', 'dp'), may hold values from -0.15625 to 0.15625
- final_gain: float32 [2048], replicated, may hold values from 0.25 to 1.75
Outputs:
- layer_out: bfloat16 [16384, 2048], P(('expert', 'dp'))
Inputs may be any that keep to these rules, and one draw needn't show every extreme that they name: `page_table`: the 4 pages of sequence s are distinct pages of group s // 4, which owns pages g * 16 to g * 16 + 15; every page belongs to exactly one sequence. `ctx_lens`: the first row of every sequence reads all 256 positions. `expert_ids`: each row names 6 distinct experts; among the 64 rows of one device (aligned blocks of 64 rows) no expert is named more than 12 times.
All inputs are finite; a program needn't handle non-finite values.
Results may differ from a plain program's by a relative error of at most 0.017.
Values may be sent and summed in bfloat16 or wider, within the bound.
A program may use at most 128 MiB of HBM per device.

v0:
```python
import math
import jax
import jax.numpy as jnp
from jax import lax
from jax.sharding import PartitionSpec as P

HD = 128
TOP = 6
CTX = 256


def normalize(values, gain):
    mean_sq = jnp.mean(values * values, axis=-1, keepdims=True)
    return values * lax.rsqrt(mean_sq + 1e-06) * gain


def fetch_experts(w_gate, w_up, w_down):
    return (
        lax.all_gather(w_gate, "dp", axis=1, tiled=True),
        lax.all_gather(w_up, "dp", axis=1, tiled=True),
        lax.all_gather(w_down, "dp", axis=1, tiled=True),
    )


def shards(
    queries,
    kv_pool,
    page_table,
    ctx_lens,
    w_out,
    residual,
    moe_gain,
    expert_ids,
    route_weights,
    w_gate,
    w_up,
    w_down,
    final_gain,
):
    replicas = None
    scale = 1.0 / math.sqrt(HD)
    group_rows = queries.shape[0]
    local_feats = queries.shape[1]
    local_heads = local_feats // HD
    seq_count = page_table.shape[0]
    seq_rows = group_rows // seq_count
    pool_here = kv_pool.shape[1]
    local_pages = page_table - lax.axis_index("expert") * pool_here
    keys = kv_pool[0][local_pages].reshape(seq_count, CTX, local_heads, HD)
    values = kv_pool[1][local_pages].reshape(seq_count, CTX, local_heads, HD)
    asked = queries.reshape(seq_count, seq_rows, local_heads, HD)
    scores = jnp.einsum("sqhd,skhd->shqk", asked, keys, preferred_element_type=jnp.float32) * scale
    lengths = ctx_lens.reshape(seq_count, seq_rows)
    visible = (jnp.arange(CTX, dtype=jnp.int32)[None, None, :] < lengths[:, :, None])[:, None]
    scores = jnp.where(visible, scores, -1e30)
    top_score = jnp.max(scores, axis=-1, keepdims=True)
    expo = jnp.where(visible, jnp.exp(scores - top_score), 0.0)
    probs = (expo / jnp.sum(expo, axis=-1, keepdims=True)).astype(jnp.bfloat16)
    mixed = jnp.einsum("shqk,skhd->sqhd", probs, values, preferred_element_type=jnp.float32)
    context = mixed.astype(jnp.bfloat16).reshape(group_rows, local_feats)
    columns = lax.all_gather(w_out, "expert", axis=1, tiled=True)
    projected = lax.psum_scatter(
        jnp.dot(context, columns, preferred_element_type=jnp.float32).astype(jnp.bfloat16),
        "dp",
        scatter_dimension=0,
        tiled=True,
    ).astype(jnp.float32)
    hidden_state = residual.astype(jnp.float32) + projected
    moe_input = normalize(hidden_state, moe_gain).astype(jnp.bfloat16)
    rows_here = moe_input.shape[0]
    experts = lax.axis_size("expert")
    slots = max(2, min(rows_here, 2 * rows_here * TOP // experts))
    flat_ids = expert_ids.reshape(-1)
    marks = (flat_ids[:, None] == jnp.arange(experts, dtype=jnp.int32)[None, :]).astype(jnp.int32)
    before = jnp.sum((jnp.cumsum(marks, axis=0) - 1) * marks, axis=1)
    target = (flat_ids * slots + before).reshape(rows_here, TOP)
    placing = jnp.any(
        jnp.arange(experts * slots, dtype=jnp.int32)[:, None, None] == target[None], axis=-1
    )
    outbound = jnp.dot(placing.astype(jnp.bfloat16), moe_input, preferred_element_type=jnp.float32)
    outbound = outbound.astype(jnp.bfloat16).reshape(experts, slots, moe_input.shape[1])
    replicas = fetch_experts(w_gate, w_up, w_down)
    gate_full, up_full, down_full = replicas
    arrived = lax.all_to_all(outbound, "expert", split_axis=0, concat_axis=0, tiled=True)
    flat = arrived.reshape(-1, arrived.shape[2])
    gate = jnp.dot(flat, gate_full[0], preferred_element_type=jnp.float32)
    up_part = jnp.dot(flat, up_full[0], preferred_element_type=jnp.float32)
    expert_mid = (jax.nn.silu(gate) * up_part).astype(jnp.bfloat16)
    done = jnp.dot(expert_mid, down_full[0], preferred_element_type=jnp.float32).astype(
        jnp.bfloat16
    )
    done = done.reshape(arrived.shape[0], arrived.shape[1], arrived.shape[2])
    returned = lax.all_to_all(done, "expert", split_axis=0, concat_axis=0, tiled=True)
    answers = returned.reshape(experts * slots, returned.shape[2])[target]
    moe = jnp.sum(route_weights[:, :, None] * answers.astype(jnp.float32), axis=1)
    combined = hidden_state + moe
    return normalize(combined, final_gain).astype(jnp.bfloat16)


def solution(mesh):
    return jax.shard_map(
        shards,
        mesh=mesh,
        in_specs=(
            P("expert", "dp"),
            P(None, "expert", None, "dp"),
            P("expert", None),
            P("expert"),
            P("dp", "expert"),
            P(("expert", "dp"), None),
            P(),
            P(("expert", "dp"), None),
            P(("expert", "dp"), None),
            P("expert", "dp", None),
            P("expert", "dp", None),
            P("expert", "dp", None),
            P(),
        ),
        out_specs=P(("expert", "dp"), None),
        check_vma=False,
    )
```

profile of v0, /device:TPU:8, one launch (start us, length us, event | category | flops | bytes accessed | tf_op | source)
XLA Modules:
  0.0 469.7 jit_solution(8235177650475701003)
XLA Ops:
  8.1 1.7 slice_bitcast_fusion
  12.7 1.6 fusion.34
  14.3 1.6 fusion.18
  16.1 73.2 %all-gather.5.cloned.1.call-done = bf16[512,2048]{0,1:T(8,128)(2,1)} async-done(((bf16[512,32]{0,1:T(8,128)(2,1)}), bf16[512,2048]{0,1:T(8,128)(2,1)}) %all-gather.5.cloned.1.call-update) | async-done | bytes 2097168 | tf_op jit(solution)/shard_map/all_gather | solution.py:61
  89.3 3.4 convolution_convert_fusion.1
  95.0 0.9 reduce-window.6
  96.8 20.8 %reduce-scatter.2.cloned.1.call-done = bf16[64,2048]{1,0:T(8,128)(2,1)} async-done(((bf16[256,2048]{1,0:T(8,128)(2,1)}), bf16[64,2048]{1,0:T(8,128)(2,1)}) %reduce-scatter.2.cloned.1.call-update) | async-done | bytes 262160 | tf_op jit(solution)/shard_map/reduce_scatter | solution.py:62
  117.6 1.1 multiply_reduce_fusion.2
  118.8 2.0 convolution_convert_fusion
  120.8 2.7 reshape.82
  123.4 106.9 %all_to_all.10 = bf16[64,12,2048]{2,1,0:T(8,128)(2,1)} all-to-all(bf16[64,12,2048]{2,1,0:T(8,128)(2,1)} %reshape.82), channel_id=1, replica_groups=mesh['dp'=4,'expert'=64] {'expert'}, dimensions={0} | all-to-all | bytes 6291456 | tf_op jit(solution)/shard_map/all_to_all | solution.py:84
  230.3 4.7 %reshape.83 = bf16[768,2048]{1,0:T(8,128)(2,1)S(1)} reshape(bf16[64,12,2048]{2,1,0:T(8,128)(2,1)} %all_to_all.10) | data formatting | bytes 6291456 | tf_op jit(solution)/shard_map/reshape | solution.py:85
  235.1 9.3 %fusion.3 = f32[768,1408]{1,0:T(8,128)} fusion(bf16[768,2048]{1,0:T(8,128)(2,1)S(1)} %reshape.83, bf16[1,2048,1408]{2,1,0:T(8,128)(2,1)} %all-gather.9.cloned.1.call-done), kind=kOutput, calls=%fused_computation.6 | convolution fusion | flops 4429185024 | bytes 13238272 | tf_op jit(solution)/shard_map/dot_general | solution.py:87
  244.4 5.2 %all-gather.11.cloned.1.call-done = bf16[1,1408,2048]{2,1,0:T(8,128)(2,1)} async-done(((bf16[1,352,2048]{2,1,0:T(8,128)(2,1)}), bf16[1,1408,2048]{2,1,0:T(8,128)(2,1)}) %all-gather.11.cloned.1.call-update) | async-done | bytes 5767184 | tf_op jit(solution)/shard_map/all_gather | solution.py:21
  249.6 66.3 %all-gather.7.cloned.1.call-done = bf16[1,2048,1408]{2,1,0:T(8,128)(2,1)} async-done(((bf16[1,512,1408]{2,1,0:T(8,128)(2,1)}), bf16[1,2048,1408]{2,1,0:T(8,128)(2,1)}) %all-gather.7.cloned.1.call-update) | async-done | bytes 5767184 | tf_op jit(solution)/shard_map/all_gather | solution.py:19
  315.9 17.6 %fusion.9 = bf16[768,2048]{1,0:T(8,128)(2,1)} fusion(bf16[1,1408,2048]{2,1,0:T(8,128)(2,1)} %all-gather.11.cloned.1.call-done, f32[768,1408]{1,0:T(8,128)} %fusion.3, bf16[768,2048]{1,0:T(8,128)(2,1)S(1)} %reshape.83, bf16[1,2048,1408]{2,1,0:T(8,128)(2,1)} %all-gather.7.cloned.1.call-done), kind=kOutput, calls=%fused_computation.13 | convolution fusion | flops 8866430976 | bytes 22151168 | tf_op jit(solution)/shard_map/dot_general | solution.py:89
  333.5 6.1 %reshape.84 = bf16[64,12,2048]{2,1,0:T(8,128)(2,1)} reshape(bf16[768,2048]{1,0:T(8,128)(2,1)} %fusion.9) | data formatting | bytes 6291456 | tf_op jit(solution)/shard_map/reshape | solution.py:92
  339.5 10.9 %all-to-all-start.1 = ((bf16[64,12,2048]{2,1,0:T(8,128)(2,1)}), bf16[64,12,2048]{2,1,0:T(8,128)(2,1)}, u32[]{:S(2)}, u32[]{:S(2)}) async-start(bf16[64,12,2048]{2,1,0:T(8,128)(2,1)} %reshape.84), calls=%async_computation.2 | async-start | bytes 8388608 | tf_op jit(solution)/shard_map/all_to_all | solution.py:93
  350.8 95.8 %all-to-all-done.1 = bf16[64,12,2048]{2,1,0:T(8,128)(2,1)} async-done(((bf16[64,12,2048]{2,1,0:T(8,128)(2,1)}), bf16[64,12,2048]{2,1,0:T(8,128)(2,1)}, u32[]{:S(2)}, u32[]{:S(2)}) %all-to-all-start.1) | async-done | bytes 3145760 | tf_op jit(solution)/shard_map/all_to_all | solution.py:93
  446.5 4.7 %reshape.85 = bf16[768,2048]{1,0:T(8,128)(2,1)S(1)} reshape(bf16[64,12,2048]{2,1,0:T(8,128)(2,1)} %all-to-all-done.1) | data formatting | bytes 6291456 | tf_op jit(solution)/shard_map/reshape | solution.py:94
  451.3 3.1 gather_fusion.2
  454.4 3.9 reshape.118
  458.3 3.7 multiply_reduce_fusion
  462.3 0.8 multiply_convert_fusion.1
  (58 shorter events, 8.2 us)
Async XLA Ops:
  6.5 82.8 %all-gather.5.cloned.1.call-start = ((), (), s32[]{:S(2)}) async-start(), calls=%async_computation.3 | async-start | bytes 2129920 | tf_op jit(solution)/shard_map/all_gather | solution.py:61
  7.3 110.3 %reduce-scatter.2.cloned.1.call-start = ((), (), s32[]{:S(2)}) async-start(), calls=%async_computation.4 | async-start | bytes 1310720 | tf_op jit(solution)/shard_map/reduce_scatter | solution.py:62
  8.1 2.7 copy-start.2
  8.1 3.5 copy-start.8
  11.6 1.1 copy-start.3
  89.3 5.3 %copy-start.4 = (s32[64,6]{0,1:T(8,128)S(1)}, s32[64,6]{0,1:T(8,128)}, u32[]{:S(2)}) copy-start(s32[64,6]{0,1:T(8,128)} %param.20) | copy-start | bytes 4612
  89.3 28.3 %copy-start = (bf16[64,2048]{1,0:T(8,128)(2,1)S(1)}, bf16[64,2048]{1,0:T(8,128)(2,1)}, u32[]{:S(2)}) copy-start(bf16[64,2048]{1,0:T(8,128)(2,1)} %param.18) | copy-start | bytes 786436
  89.3 29.4 %copy-start.5 = (f32[2048]{0:T(1024)S(1)}, f32[2048]{0:T(1024)}, u32[]{:S(2)}) copy-start(f32[2048]{0:T(1024)} %param.19) | copy-start | bytes 24580
  92.7 142.3 %all-gather.9.cloned.1.call-start = ((), (), s32[]{:S(2)}) async-start(), calls=%async_computation.6 | async-start | bytes 7208960 | tf_op jit(solution)/shard_map/all_gather | solution.py:20
  93.5 156.1 %all-gather.11.cloned.1.call-start = ((), (), s32[]{:S(2)}) async-start(), calls=%async_computation.7 | async-start | bytes 7208960 | tf_op jit(solution)/shard_map/all_gather | solution.py:21
  94.0 221.8 %all-gather.7.cloned.1.call-start = ((), (), s32[]{:S(2)}) async-start(), calls=%async_computation.5 | async-start | bytes 7208960 | tf_op jit(solution)/shard_map/all_gather | solution.py:19
  339.5 11.1 %copy-start.7 = (f32[64,6]{0,1:T(8,128)S(1)}, f32[64,6]{0,1:T(8,128)}, u32[]{:S(2)}) copy-start(f32[64,6]{0,1:T(8,128)} %param.21) | copy-start | bytes 4612
  339.5 107.0 %all-to-all-start.1 = ((bf16[64,12,2048]{2,1,0:T(8,128)(2,1)}), bf16[64,12,2048]{2,1,0:T(8,128)(2,1)}, u32[]{:S(2)}, u32[]{:S(2)}) async-start(bf16[64,12,2048]{2,1,0:T(8,128)(2,1)} %reshape.84), calls=%async_computation.2 | async-start | bytes 8388608 | tf_op jit(solution)/shard_map/all_to_all | solution.py:93
  454.4 7.7 %copy-start.1 = (bf16[64,2048]{1,0:T(8,128)(2,1)S(1)}, bf16[64,2048]{1,0:T(8,128)(2,1)}, u32[]{:S(2)}) copy-start(bf16[64,2048]{1,0:T(8,128)(2,1)} %reduce-scatter.2.cloned.1.call-done) | copy-start | bytes 786436
  458.3 4.0 copy-start.6
Sparse Core Ops, SparseCore 0:
  10.1 79.1 all-gather.4
  92.8 24.6 reduce-scatter.1
  119.6 63.6 all-gather.8
  185.1 64.4 all-gather.10
  251.4 64.4 all-gather.6
where the time goes:
time: 471 us; the launch traced here: 470 us
  waiting for transfers between devices  264 us (56%)
  blocking collectives  107 us (23%)
  matrix products  35.4 us (8%)
  local copies, waits for them, and re-layouts  31.1 us (7%)
  between operations  13.4 us (3%)
  starting transfers between devices  11 us (2%)
  other arithmetic  8.07 us (2%)
    all_to_all x1, blocking collectives, shards(): lax.all_to_all(outbound, 'expert', split_axis=0, concat_axis=0, tiled=True)  107 us
    all_to_all x1, waiting for transfers between devices, shards(): lax.all_to_all(done, 'expert', split_axis=0, concat_axis=0, tiled=True)  95.8 us
    all_gather x1, waiting for transfers between devices, shards(): columns = lax.all_gather(w_out, 'expert', axis=1, tiled=True)  73.2 us
    all_gather x1, waiting for transfers between devices, fetch_experts(): lax.all_gather(w_gate, 'dp', axis=1, tiled=True)  66.3 us
    reduce_scatter x1, waiting for transfers between devices, shards(): lax.psum_scatter(jnp.dot(context, columns, preferred_element_type=jnp.flo...  20.8 us
    dot_general x1, matrix products, shards(): jnp.dot(expert_mid, down_full[0], preferred_element_type=jnp.float32)  17.6 us
    all_to_all x1, starting transfers between devices, shards(): lax.all_to_all(done, 'expert', split_axis=0, concat_axis=0, tiled=True)  10.9 us
  transfers between devices with their start and end apart: 6, of which 5 were waited for; matrix products, arithmetic and copies ran while one was open for 7% of the time, Pallas kernels for 0%

commit v1 on v0

--- a/solution.py
+++ b/solution.py
@@ -9,6 +9,19 @@
 CTX = 256
 
 
+def ring_gather(value, axis, dim):
+    ways = lax.axis_size(axis)
+    up = [(d, (d + 1) % ways) for d in range(ways)]
+    down = [(d, (d - 1) % ways) for d in range(ways)]
+    earlier, later = ([value], [value])
+    for _ in range(ways // 2):
+        earlier.append(lax.ppermute(earlier[-1], axis, up))
+    for _ in range((ways - 1) // 2):
+        later.append(lax.ppermute(later[-1], axis, down))
+    line = jnp.concatenate([*earlier[::-1], *later[1:]], axis=dim)
+    return jnp.roll(line, (lax.axis_index(axis) - ways // 2) * value.shape[dim], axis=dim)
+
+
 def normalize(values, gain):
     mean_sq = jnp.mean(values * values, axis=-1, keepdims=True)
     return values * lax.rsqrt(mean_sq + 1e-06) * gain
@@ -16,7 +29,7 @@
 
 def fetch_experts(w_gate, w_up, w_down):
     return (
-        lax.all_gather(w_gate, "dp", axis=1, tiled=True),
+        ring_gather(w_gate, "dp", 1),
         lax.all_gather(w_up, "dp", axis=1, tiled=True),
         lax.all_gather(w_down, "dp", axis=1, tiled=True),
     )

time: 471 us -> 446 us (0.947)
  blocking collectives: 107 us -> 0 us
  waiting for transfers between devices: 264 us -> 316 us
  local copies, waits for them, and re-layouts: 31.1 us -> 46.5 us
  starting transfers between devices: 11 us -> 25.2 us
    ppermute x0 -> x3, waiting for transfers between devices: none -> 107 us  [the longest x2 107 us: ring_gather(): earlier.append(lax.ppermute(earlier[-1], axis, up))]
    all_to_all x1 -> x0, blocking collectives: 107 us -> none  [shards(): lax.all_to_all(outbound, 'expert', split_axis=0, concat_axis=0, tiled=True)]
    all_gather x1 -> x0, waiting for transfers between devices: 66.3 us -> none  [fetch_experts(): lax.all_gather(w_gate, 'dp', axis=1, tiled=True)]
    unnamed x20 -> x27, local copies, waits for them, and re-layouts: 0.23 us -> 13 us
    all_gather x1, waiting for transfers between devices: 5.21 us -> 17.2 us  [fetch_experts(): lax.all_gather(w_down, 'dp', axis=1, tiled=True)]
    all_to_all x0 -> x1, starting transfers between devices: none -> 10.8 us  [shards(): lax.all_to_all(outbound, 'expert', split_axis=0, concat_axis=0, tiled=True)]
  transfers between devices with their start and end apart: 6 -> 9, of which waited for: 5 -> 6; matrix products, arithmetic and copies ran while one was open for 7% -> 11% of each run, Pallas kernels for 0% -> 0%
where the time goes in v1:
time: 446 us; the launch traced here: 445 us
  waiting for transfers between devices  316 us (71%)
  local copies, waits for them, and re-layouts  46.5 us (10%)
  matrix products  36.3 us (8%)
  starting transfers between devices  25.2 us (6%)
  between operations  13.4 us (3%)
  other arithmetic  8.07 us (2%)
    ppermute x2, waiting for transfers between devices, ring_gather(): earlier.append(lax.ppermute(earlier[-1], axis, up))  107 us
    all_to_all x1, waiting for transfers between devices, shards(): lax.all_to_all(done, 'expert', split_axis=0, concat_axis=0, tiled=True)  95.8 us
    all_gather x1, waiting for transfers between devices, shards(): columns = lax.all_gather(w_out, 'expert', axis=1, tiled=True)  72.3 us
    reduce_scatter x1, waiting for transfers between devices, shards(): lax.psum_scatter(jnp.dot(context, columns, preferred_element_type=jnp.flo...  21.4 us
    dot_general x1, matrix products, shards(): jnp.dot(expert_mid, down_full[0], preferred_element_type=jnp.float32)  17.5 us
    all_gather x1, waiting for transfers between devices, fetch_experts(): lax.all_gather(w_down, 'dp', axis=1, tiled=True)  17.2 us
    unnamed x27, local copies, waits for them, and re-layouts  13 us
    all_to_all x1, starting transfers between devices, shards(): lax.all_to_all(done, 'expert', split_axis=0, concat_axis=0, tiled=True)  10.9 us
  transfers between devices with their start and end apart: 9, of which 6 were waited for; matrix products, arithmetic and copies ran while one was open for 11% of the time, Pallas kernels for 0%

profile of v1, /device:TPU:8, one launch (start us, length us, event | category | flops | bytes accessed | tf_op | source)
XLA Modules:
  0.0 445.0 jit_solution(4434382338128806184)
XLA Ops:
  12.6 2.6 fusion.37
  17.0 72.3 %all-gather.4.cloned.1.call-done = bf16[512,2048]{0,1:T(8,128)(2,1)} async-done(((bf16[512,32]{0,1:T(8,128)(2,1)}), bf16[512,2048]{0,1:T(8,128)(2,1)}) %all-gather.4.cloned.1.call-update) | async-done | bytes 2097168 | tf_op jit(solution)/shard_map/all_gather | solution.py:74
  89.3 3.3 convolution_convert_fusion.1
  96.2 21.4 %reduce-scatter.2.cloned.1.call-done = bf16[64,2048]{1,0:T(8,128)(2,1)} async-done(((bf16[256,2048]{1,0:T(8,128)(2,1)}), bf16[64,2048]{1,0:T(8,128)(2,1)}) %reduce-scatter.2.cloned.1.call-update) | async-done | bytes 262160 | tf_op jit(solution)/shard_map/reduce_scatter | solution.py:75
  120.8 2.7 reshape.82
  123.5 10.8 %all-to-all-start = ((bf16[64,12,2048]{2,1,0:T(8,128)(2,1)}), bf16[64,12,2048]{2,1,0:T(8,128)(2,1)}, u32[]{:S(2)}, u32[]{:S(2)}) async-start(bf16[64,12,2048]{2,1,0:T(8,128)(2,1)} %reshape.82), calls=%async_computation.1 | async-start | bytes 8388608 | tf_op jit(solution)/shard_map/all_to_all | solution.py:97
  134.4 66.2 %collective-permute-done = bf16[1,512,1408]{2,1,0:T(8,128)(2,1)S(1)} collective-permute-done((bf16[1,512,1408]{2,1,0:T(8,128)(2,1)S(1)}, bf16[1,512,1408]{2,1,0:T(8,128)(2,1)S(1)}, u32[]{:S(2)}, u32[]{:S(2)}) %collective-permute-start) | collective-permute-done | bytes 1441824 | tf_op jit(solution)/shard_map/ppermute | solution.py:18
  200.7 3.2 collective-permute-start.2
  203.9 40.8 %collective-permute-done.1 = bf16[1,512,1408]{2,1,0:T(8,128)(2,1)} collective-permute-done((bf16[1,512,1408]{2,1,0:T(8,128)(2,1)S(1)}, bf16[1,512,1408]{2,1,0:T(8,128)(2,1)}, u32[]{:S(2)}, u32[]{:S(2)}) %collective-permute-start.1) | collective-permute-done | bytes 1441824 | tf_op jit(solution)/shard_map/ppermute | solution.py:18
  244.7 2.6 constant_dynamic-update-slice_fusion.7
  249.7 2.6 constant_dynamic-update-slice_fusion.4
  252.4 2.6 constant_dynamic-update-slice_fusion.3
  257.5 2.6 constant_dynamic-update-slice_fusion
  260.1 4.7 %reshape.83 = bf16[768,2048]{1,0:T(8,128)(2,1)S(1)} reshape(bf16[64,12,2048]{2,1,0:T(8,128)(2,1)} %all-to-all-done) | data formatting | bytes 6291456 | tf_op jit(solution)/shard_map/reshape | solution.py:98
  264.8 9.3 %fusion.3 = f32[768,1408]{1,0:T(8,128)} fusion(bf16[768,2048]{1,0:T(8,128)(2,1)S(1)} %reshape.83, bf16[1,2048,1408]{2,1,0:T(8,128)(2,1)} %all-gather.6.cloned.1.call-done), kind=kOutput, calls=%fused_computation.6 | convolution fusion | flops 4429185024 | bytes 13238272 | tf_op jit(solution)/shard_map/dot_general | solution.py:100
  274.2 17.2 %all-gather.8.cloned.1.call-done = bf16[1,1408,2048]{2,1,0:T(8,128)(2,1)} async-done(((bf16[1,352,2048]{2,1,0:T(8,128)(2,1)}), bf16[1,1408,2048]{2,1,0:T(8,128)(2,1)}) %all-gather.8.cloned.1.call-update) | async-done | bytes 5767184 | tf_op jit(solution)/shard_map/all_gather | solution.py:34
  291.3 17.5 %fusion.10 = bf16[768,2048]{1,0:T(8,128)(2,1)} fusion(bf16[1,1408,2048]{2,1,0:T(8,128)(2,1)} %all-gather.8.cloned.1.call-done, f32[768,1408]{1,0:T(8,128)} %fusion.3, bf16[768,2048]{1,0:T(8,128)(2,1)S(1)} %reshape.83, bf16[1,4096,1408]{2,1,0:T(8,128)(2,1)} %constant_dynamic-update-slice_fusion, s32[]{:T(128)S(6)} %select_n.31), kind=kOutput, calls=%fused_computation.14 | convolution fusion | flops 8866430976 | bytes 22151172 | tf_op jit(solution)/shard_map/dot_general | solution.py:102
  308.8 6.1 %reshape.84 = bf16[64,12,2048]{2,1,0:T(8,128)(2,1)} reshape(bf16[768,2048]{1,0:T(8,128)(2,1)} %fusion.10) | data formatting | bytes 6291456 | tf_op jit(solution)/shard_map/reshape | solution.py:105
  314.9 10.9 %all-to-all-start.1 = ((bf16[64,12,2048]{2,1,0:T(8,128)(2,1)}), bf16[64,12,2048]{2,1,0:T(8,128)(2,1)}, u32[]{:S(2)}, u32[]{:S(2)}) async-start(bf16[64,12,2048]{2,1,0:T(8,128)(2,1)} %reshape.84), calls=%async_computation.2 | async-start | bytes 8388608 | tf_op jit(solution)/shard_map/all_to_all | solution.py:106
  326.1 95.8 %all-to-all-done.1 = bf16[64,12,2048]{2,1,0:T(8,128)(2,1)} async-done(((bf16[64,12,2048]{2,1,0:T(8,128)(2,1)}), bf16[64,12,2048]{2,1,0:T(8,128)(2,1)}, u32[]{:S(2)}, u32[]{:S(2)}) %all-to-all-start.1) | async-done | bytes 3145760 | tf_op jit(solution)/shard_map/all_to_all | solution.py:106
  421.9 4.7 %reshape.85 = bf16[768,2048]{1,0:T(8,128)(2,1)S(1)} reshape(bf16[64,12,2048]{2,1,0:T(8,128)(2,1)} %all-to-all-done.1) | data formatting | bytes 6291456 | tf_op jit(solution)/shard_map/reshape | solution.py:107
  426.6 3.1 gather_fusion.2
  429.7 3.9 reshape.118
  433.7 3.7 multiply_reduce_fusion
  (70 shorter events, 20.9 us)
Async XLA Ops:
  6.5 4.2 copy-start.3
  6.5 82.8 %all-gather.4.cloned.1.call-start = ((), (), s32[]{:S(2)}) async-start(), calls=%async_computation.3 | async-start | bytes 2129920 | tf_op jit(solution)/shard_map/all_gather | solution.py:74
  7.3 110.3 %reduce-scatter.2.cloned.1.call-start = ((), (), s32[]{:S(2)}) async-start(), calls=%async_computation.4 | async-start | bytes 1310720 | tf_op jit(solution)/shard_map/reduce_scatter | solution.py:75
  8.1 3.4 copy-start.8
  16.8 77.2 %copy-start.4 = (s32[64,6]{0,1:T(8,128)S(1)}, s32[64,6]{0,1:T(8,128)}, u32[]{:S(2)}) copy-start(s32[64,6]{0,1:T(8,128)} %param.20) | copy-start | bytes 4612
  16.8 100.8 %copy-start.1 = (bf16[64,2048]{1,0:T(8,128)(2,1)S(1)}, bf16[64,2048]{1,0:T(8,128)(2,1)}, u32[]{:S(2)}) copy-start(bf16[64,2048]{1,0:T(8,128)(2,1)} %param.18) | copy-start | bytes 786436
  17.0 101.7 %copy-start.5 = (f32[2048]{0:T(1024)S(1)}, f32[2048]{0:T(1024)}, u32[]{:S(2)}) copy-start(f32[2048]{0:T(1024)} %param.19) | copy-start | bytes 24580
  92.7 172.2 %all-gather.6.cloned.1.call-start = ((), (), s32[]{:S(2)}) async-start(), calls=%async_computation.5 | async-start | bytes 7208960 | tf_op jit(solution)/shard_map/all_gather | solution.py:33
  93.4 197.9 %all-gather.8.cloned.1.call-start = ((), (), s32[]{:S(2)}) async-start(), calls=%async_computation.6 | async-start | bytes 7208960 | tf_op jit(solution)/shard_map/all_gather | solution.py:34
  123.5 10.8 %copy-start = (bf16[1,512,1408]{2,1,0:T(8,128)(2,1)S(1)}, bf16[1,512,1408]{2,1,0:T(8,128)(2,1)}, u32[]{:S(2)}) copy-start(bf16[1,512,1408]{2,1,0:T(8,128)(2,1)} %param.22) | copy-start | bytes 4325380
  123.5 136.6 %all-to-all-start = ((bf16[64,12,2048]{2,1,0:T(8,128)(2,1)}), bf16[64,12,2048]{2,1,0:T(8,128)(2,1)}, u32[]{:S(2)}, u32[]{:S(2)}) async-start(bf16[64,12,2048]{2,1,0:T(8,128)(2,1)} %reshape.82), calls=%async_computation.1 | async-start | bytes 8388608 | tf_op jit(solution)/shard_map/all_to_all | solution.py:97
  134.3 66.3 %collective-permute-start = (bf16[1,512,1408]{2,1,0:T(8,128)(2,1)S(1)}, bf16[1,512,1408]{2,1,0:T(8,128)(2,1)S(1)}, u32[]{:S(2)}, u32[]{:S(2)}) collective-permute-start(bf16[1,512,1408]{2,1,0:T(8,128)(2,1)S(1)} %copy-done), channel_id=1, source_target_pairs={{0,64},{64,128},{128,192},{192,0},{1,65},{65,129},{129,193},{193,1... | collective-permute-start | bytes 4325384 | tf_op jit(solution)/shard_map/ppermute | solution.py:18
  200.7 44.0 %collective-permute-start.1 = (bf16[1,512,1408]{2,1,0:T(8,128)(2,1)S(1)}, bf16[1,512,1408]{2,1,0:T(8,128)(2,1)}, u32[]{:S(2)}, u32[]{:S(2)}) collective-permute-start(bf16[1,512,1408]{2,1,0:T(8,128)(2,1)S(1)} %collective-permute-done), channel_id=1, source_target_pairs={{0,64},{64,128},{128,192},{192,0},{1,65},{65,129},{129,193},{193,1... | collective-permute-start | bytes 4325384 | tf_op jit(solution)/shard_map/ppermute | solution.py:18
  200.7 49.1 %collective-permute-start.2 = (bf16[1,512,1408]{2,1,0:T(8,128)(2,1)S(1)}, bf16[1,512,1408]{2,1,0:T(8,128)(2,1)}, u32[]{:S(2)}, u32[]{:S(2)}) collective-permute-start(bf16[1,512,1408]{2,1,0:T(8,128)(2,1)S(1)} %copy-done), channel_id=1, source_target_pairs={{0,192},{64,0},{128,64},{192,128},{1,193},{65,1},{129,65},{193,129... | collective-permute-start | bytes 4325384 | tf_op jit(solution)/shard_map/ppermute | solution.py:20
  314.9 11.1 %copy-start.7 = (f32[64,6]{0,1:T(8,128)S(1)}, f32[64,6]{0,1:T(8,128)}, u32[]{:S(2)}) copy-start(f32[64,6]{0,1:T(8,128)} %param.21) | copy-start | bytes 4612
  314.9 107.0 %all-to-all-start.1 = ((bf16[64,12,2048]{2,1,0:T(8,128)(2,1)}), bf16[64,12,2048]{2,1,0:T(8,128)(2,1)}, u32[]{:S(2)}, u32[]{:S(2)}) async-start(bf16[64,12,2048]{2,1,0:T(8,128)(2,1)} %reshape.84), calls=%async_computation.2 | async-start | bytes 8388608 | tf_op jit(solution)/shard_map/all_to_all | solution.py:106
  429.7 7.7 %copy-start.2 = (bf16[64,2048]{1,0:T(8,128)(2,1)S(1)}, bf16[64,2048]{1,0:T(8,128)(2,1)}, u32[]{:S(2)}) copy-start(bf16[64,2048]{1,0:T(8,128)(2,1)} %reduce-scatter.2.cloned.1.call-done) | copy-start | bytes 786436
  433.7 4.0 copy-start.6
Sparse Core Ops, SparseCore 0:
  10.1 79.1 all-gather.3
  92.8 24.7 reduce-scatter.1
  119.6 104.0 all-gather.5
  225.4 65.8 all-gather.7
